TPU v7x, 32 devices: a whole 2x2x4 slice. The times are simulated.
32 devices in a mesh: dp: 8 (over z, x), head: 4 (over y, core).
Axes of the slice: x: 2, y: 2, z: 4, core: 2. Of those that a mesh axis runs over, the one named last changes fastest.
Arguments:
- input_segments: float32 [16384, 32], P(('dp', 'head')), may hold values from -6 to 6
- filler_flags: int32 [16384, 32], P(('dp', 'head')), may hold values 0 or 1
- sequence_owner: int32 [16384], P(('dp', 'head')), may hold values from 0 to 127, never falling along the last dimension, each value on 1 to 256 neighbouring positions
- prediction_adjoint: bfloat16 [16384, 1280], P('dp', 'head'), may hold values from -6 to 6
- quadratic_params: float32 [6, 1280, 1280], P(None, ('dp', 'head')), may hold values from -0.3354102 to 0.3354102, as said below
- quadratic_velocity: float32 [6, 1280, 1280], P(None, ('dp', 'head')), may hold values from -384 to 384
- quadratic_mean: float32 [6, 1280, 1280], P(None, ('dp', 'head')), may hold values from -0.15625 to 0.15625
- perceptron_params: float32 [2, 1280, 5120], P(None, ('dp', 'head')), may hold values from -0.15625 to 0.15625
- perceptron_velocity: float32 [2, 1280, 5120], P(None, ('dp', 'head')), may hold values from -384 to 384
- perceptron_mean: float32 [2, 1280, 5120], P(None, ('dp', 'head')), may hold values from -0.15625 to 0.15625
- embedder_params: float32 [2, 1280, 64], P(None, ('dp', 'head')), may hold values from -0.75 to 0.75
- embedder_velocity: float32 [2, 1280, 64], P(None, ('dp', 'head')), may hold values from -384 to 384
- embedder_mean: float32 [2, 1280, 64], P(None, ('dp', 'head')), may hold values from -0.75 to 0.75
- bias_gain_params: float32 [5, 1280], P(None, ('dp', 'head')), may hold values from -1.6 to 1.6, as said below
- bias_gain_velocity: float32 [5, 1280], P(None, ('dp', 'head')), may hold values from -384 to 384
- bias_gain_mean: float32 [5, 1280], P(None, ('dp', 'head')), may hold values from -1.6 to 1.6, as said below
- readout_params: float32 [2, 1280, 1280], P(None, 'dp', 'head'), may hold values from -0.15625 to 0.15625
- readout_velocity: float32 [2, 1280, 1280], P(None, 'dp', 'head'), may hold values from -384 to 384
- readout_mean: float32 [2, 1280, 1280], P(None, 'dp', 'head'), may hold values from -0.15625 to 0.15625
Outputs:
- prediction: bfloat16 [16384, 1280], P('dp', 'head')
- segment_derivative: float32 [16384, 32], P(('dp', 'head'))
- quadratic_params_fresh: float32 [6, 1280, 1280], P(None, ('dp', 'head'))
- quadratic_velocity_fresh: float32 [6, 1280, 1280], P(None, ('dp', 'head'))
- quadratic_mean_fresh: float32 [6, 1280, 1280], P(None, ('dp', 'head'))
- perceptron_params_fresh: float32 [2, 1280, 5120], P(None, ('dp', 'head'))
- perceptron_velocity_fresh: float32 [2, 1280, 5120], P(None, ('dp', 'head'))
- perceptron_mean_fresh: float32 [2, 1280, 5120], P(None, ('dp', 'head'))
- embedder_params_fresh: float32 [2, 1280, 64], P(None, ('dp', 'head'))
- embedder_velocity_fresh: float32 [2, 1280, 64], P(None, ('dp', 'head'))
- embedder_mean_fresh: float32 [2, 1280, 64], P(None, ('dp', 'head'))
- bias_gain_params_fresh: float32 [5, 1280], P(None, ('dp', 'head'))
- bias_gain_velocity_fresh: float32 [5, 1280], P(None, ('dp', 'head'))
- bias_gain_mean_fresh: float32 [5, 1280], P(None, ('dp', 'head'))
- readout_params_fresh: float32 [2, 1280, 1280], P(None, 'dp', 'head')
- readout_velocity_fresh: float32 [2, 1280, 1280], P(None, 'dp', 'head')
- readout_mean_fresh: float32 [2, 1280, 1280], P(None, 'dp', 'head')
Inputs may be any that keep to these rules, and one draw needn't show every extreme that they name: quadratic_params entries lie within this range. bias_gain_params entries lie within this range. bias_gain_mean entries lie within this range.
All inputs are finite; a program needn't handle non-finite values. No bound on the sum of `filler_flags` on one device may be relied on, other than what follows from the above.
Results may differ from a plain program's by a relative error of at most 0.019.
Values may be sent and summed in bfloat16 or wider, within the bound.
A program may use at most 448 MiB of HBM per device.

v0:
```python
import jax
import jax.numpy as jnp
from jax import lax
from jax.sharding import PartitionSpec as P

D = 1280
HEADS = 16
HEAD_DIM = 80
PATCH = 32
SEQ = 512
EPSILON = 1e-06
MOMENTUM = 0.9
AVG_DECAY = 0.9


def matrix_multiply(left_mat, right_mat):
    return jnp.dot(left_mat, right_mat, preferred_element_type=jnp.float32)


def flipped_bilinear(left_mat, right_mat):
    return lax.dot_general(
        left_mat, right_mat, (((1,), (1,)), ((), ())), preferred_element_type=jnp.float32
    )


def bilinear_flipped(left_mat, right_mat):
    return lax.dot_general(
        left_mat, right_mat, (((0,), (0,)), ((), ())), preferred_element_type=jnp.float32
    )


def rounded(values_in):
    return values_in.astype(jnp.bfloat16)


def rms_gain(values_in, gains_in):
    return (
        values_in
        * lax.rsqrt(jnp.mean(values_in * values_in, axis=-1, keepdims=True) + EPSILON)
        * gains_in
    )


def silu_slope(values_in):
    logistic = jax.nn.sigmoid(values_in)
    return logistic * (1.0 + values_in * (1.0 - logistic))


def rope_tables():
    half_dim = HEAD_DIM // 2
    position = jnp.arange(SEQ, dtype=jnp.float32)[:, None]
    spacing = 10000.0 ** (-jnp.arange(half_dim, dtype=jnp.float32) / half_dim)
    angles = position * spacing[None, :]
    return (jnp.cos(angles), jnp.sin(angles))


def rotate(heads_in, cosines, sines):
    half_dim = heads_in.shape[-1] // 2
    lower_half = heads_in[..., :half_dim]
    upper_half = heads_in[..., half_dim:]
    cos_rows = cosines[:, None, :]
    sin_rows = sines[:, None, :]
    return jnp.concatenate(
        [
            lower_half * cos_rows - upper_half * sin_rows,
            upper_half * cos_rows + lower_half * sin_rows,
        ],
        axis=-1,
    )


def masked_scores(query_heads, key_heads, segments):
    scores = jnp.einsum(
        "qhd,khd->hqk", query_heads, key_heads, preferred_element_type=jnp.float32
    ) * HEAD_DIM ** (-0.5)
    places = jnp.arange(SEQ)
    allowed = (places[:, None] >= places[None, :]) & (segments[:, None] == segments[None, :])
    return jnp.where(allowed[None], scores, -1e30)


def attend(bundle):
    query_heads, key_heads, value_heads, segments = bundle
    scores = masked_scores(query_heads, key_heads, segments)
    row_max = jnp.max(scores, axis=-1, keepdims=True)
    expo = jnp.exp(scores - row_max)
    row_total = jnp.sum(expo, axis=-1, keepdims=True)
    probability = expo / row_total
    mixed = jnp.einsum(
        "hqk,khd->qhd", rounded(probability), value_heads, preferred_element_type=jnp.float32
    )
    return (rounded(mixed), (row_max + jnp.log(row_total))[..., 0])


def attend_back(bundle):
    query_heads, key_heads, value_heads, segments, log_totals, grad_mixed = bundle
    scores = masked_scores(query_heads, key_heads, segments)
    probability = jnp.exp(scores - log_totals[..., None])
    grad_probs = jnp.einsum(
        "qhd,khd->hqk", grad_mixed, value_heads, preferred_element_type=jnp.float32
    )
    grad_values = jnp.einsum(
        "hqk,qhd->khd", rounded(probability), grad_mixed, preferred_element_type=jnp.float32
    )
    inner_sum = jnp.sum(probability * grad_probs, axis=-1, keepdims=True)
    grad_scores = rounded(probability * (grad_probs - inner_sum))
    grad_queries = jnp.einsum(
        "hqk,khd->qhd", grad_scores, key_heads, preferred_element_type=jnp.float32
    ) * HEAD_DIM ** (-0.5)
    grad_keys = jnp.einsum(
        "hqk,qhd->khd", grad_scores, query_heads, preferred_element_type=jnp.float32
    ) * HEAD_DIM ** (-0.5)
    return (grad_queries, grad_keys, grad_values)


def update(master, moment, average, gradient, rate):
    moment_new = MOMENTUM * moment + gradient
    master_new = master - rate * (gradient + MOMENTUM * moment_new)
    average_new = AVG_DECAY * average + (1.0 - AVG_DECAY) * master_new
    return (master_new, moment_new, average_new)


def on_device(
    input_segments,
    filler_flags,
    sequence_owner,
    prediction_adjoint,
    quadratic_params,
    quadratic_velocity,
    quadratic_mean,
    perceptron_params,
    perceptron_velocity,
    perceptron_mean,
    embedder_params,
    embedder_velocity,
    embedder_mean,
    bias_gain_params,
    bias_gain_velocity,
    bias_gain_mean,
    readout_params,
    readout_velocity,
    readout_mean,
):
    square, ffn, token, vector_low = (
        lax.all_gather(rounded(quadratic_params), ("dp", "head"), axis=1, tiled=True),
        lax.all_gather(rounded(perceptron_params), ("dp", "head"), axis=1, tiled=True),
        lax.all_gather(rounded(embedder_params), ("dp", "head"), axis=1, tiled=True),
        lax.all_gather(rounded(bias_gain_params), ("dp", "head"), axis=1, tiled=True),
    )
    readout_outcome = lax.all_gather(rounded(readout_params), "dp", axis=1, tiled=True)
    vectors = vector_low.astype(jnp.float32)
    tok_count = input_segments.shape[0]
    seq_rows = tok_count // SEQ
    mask_float = filler_flags.astype(jnp.float32)
    tok_input = rounded(jnp.concatenate([input_segments * (1.0 - mask_float), mask_float], axis=1))
    tok_pre = flipped_bilinear(tok_input, token[0]) + vectors[2]
    tok_act = rounded(jax.nn.silu(tok_pre))
    stream_in = (
        matrix_multiply(tok_act, square[0]) + flipped_bilinear(tok_input, token[1]) + vectors[3]
    )
    normed_one, norm_pull_one = jax.vjp(rms_gain, stream_in, vectors[0])
    normed_attn = rounded(normed_one)
    cosines, sines = rope_tables()
    query_heads = rounded(
        rotate(
            matrix_multiply(normed_attn, square[1]).reshape(seq_rows, SEQ, HEADS, HEAD_DIM),
            cosines,
            sines,
        )
    )
    key_heads = rounded(
        rotate(
            matrix_multiply(normed_attn, square[2]).reshape(seq_rows, SEQ, HEADS, HEAD_DIM),
            cosines,
            sines,
        )
    )
    value_heads = rounded(matrix_multiply(normed_attn, square[3])).reshape(
        seq_rows, SEQ, HEADS, HEAD_DIM
    )
    seg_rows = sequence_owner.reshape(seq_rows, SEQ)
    mixed, log_totals = lax.map(attend, (query_heads, key_heads, value_heads, seg_rows))
    attn_mix = mixed.reshape(tok_count, D)
    stream_mid = stream_in + matrix_multiply(attn_mix, square[4])
    normed_two, norm_pull_two = jax.vjp(rms_gain, stream_mid, vectors[1])
    normed_ffn = rounded(normed_two)
    ffn_pre = matrix_multiply(normed_ffn, ffn[0])
    ffn_act = rounded(jax.nn.silu(ffn_pre))
    stream_out = stream_mid + flipped_bilinear(ffn_act, ffn[1])
    stream_low = rounded(stream_out)
    head_pre = matrix_multiply(stream_low, square[5]) + vectors[4]
    head_act = rounded(jax.nn.silu(head_pre))
    shortcut_complete, readout_complete = (
        lax.all_gather(stream_low, "head", axis=0, tiled=True),
        lax.all_gather(head_act, "head", axis=0, tiled=True),
    )
    prediction = (
        matrix_multiply(readout_complete, readout_outcome[0])
        + matrix_multiply(shortcut_complete, readout_outcome[1])
    ).astype(jnp.bfloat16)
    gradient_of_head = jnp.stack(
        [
            bilinear_flipped(readout_complete, prediction_adjoint),
            bilinear_flipped(shortcut_complete, prediction_adjoint),
        ]
    )
    grad_head_act, grad_skip = (
        lax.psum_scatter(
            flipped_bilinear(prediction_adjoint, readout_outcome[0]).astype(jnp.bfloat16),
            "head",
            scatter_dimension=0,
            tiled=True,
        ).astype(jnp.float32),
        lax.psum_scatter(
            flipped_bilinear(prediction_adjoint, readout_outcome[1]).astype(jnp.bfloat16),
            "head",
            scatter_dimension=0,
            tiled=True,
        ).astype(jnp.float32),
    )
    grad_head_pre = rounded(grad_head_act * silu_slope(head_pre))
    grad_bias_head = jnp.sum(grad_head_pre.astype(jnp.float32), axis=0)
    grad_wh = bilinear_flipped(stream_low, grad_head_pre)
    grad_stream_out = grad_skip + flipped_bilinear(grad_head_pre, square[5])
    grad_ffn_out = rounded(grad_stream_out)
    grad_down = bilinear_flipped(grad_ffn_out, ffn_act)
    grad_ffn_pre = rounded(matrix_multiply(grad_ffn_out, ffn[1]) * silu_slope(ffn_pre))
    grad_up = bilinear_flipped(normed_ffn, grad_ffn_pre)
    grad_stream_norm, grad_gain_two = norm_pull_two(flipped_bilinear(grad_ffn_pre, ffn[0]))
    grad_stream_mid = grad_stream_out + grad_stream_norm
    grad_ffn = jnp.stack([grad_up, grad_down])
    grad_attn_out = rounded(grad_stream_mid)
    grad_wo = bilinear_flipped(attn_mix, grad_attn_out)
    grad_attn_mix = rounded(flipped_bilinear(grad_attn_out, square[4])).reshape(
        seq_rows, SEQ, HEADS, HEAD_DIM
    )
    grad_queries, grad_keys, grad_values = lax.map(
        attend_back, (query_heads, key_heads, value_heads, seg_rows, log_totals, grad_attn_mix)
    )
    grad_q_pre = rounded(rotate(grad_queries, cosines, -sines).reshape(tok_count, D))
    grad_k_pre = rounded(rotate(grad_keys, cosines, -sines).reshape(tok_count, D))
    grad_v_pre = rounded(grad_values.reshape(tok_count, D))
    grad_wq = bilinear_flipped(normed_attn, grad_q_pre)
    grad_wk = bilinear_flipped(normed_attn, grad_k_pre)
    grad_wv = bilinear_flipped(normed_attn, grad_v_pre)
    grad_normed = (
        flipped_bilinear(grad_q_pre, square[1])
        + flipped_bilinear(grad_k_pre, square[2])
        + flipped_bilinear(grad_v_pre, square[3])
    )
    grad_stream_first, grad_gain_one = norm_pull_one(grad_normed)
    grad_stream_in = grad_stream_mid + grad_stream_first
    grad_bias_out = jnp.sum(grad_stream_in, axis=0)
    grad_tok_out = rounded(grad_stream_in)
    grad_wb = bilinear_flipped(tok_act, grad_tok_out)
    grad_skip_tok = bilinear_flipped(grad_tok_out, tok_input)
    grad_tok_pre = rounded(flipped_bilinear(grad_tok_out, square[0]) * silu_slope(tok_pre))
    grad_bias_tok = jnp.sum(grad_tok_pre.astype(jnp.float32), axis=0)
    grad_hidden_tok = bilinear_flipped(grad_tok_pre, tok_input)
    grad_input = matrix_multiply(grad_tok_out, token[1]) + matrix_multiply(grad_tok_pre, token[0])
    segment_derivative = grad_input[:, :PATCH] * (1.0 - mask_float)
    grad_square = jnp.stack([grad_wb, grad_wq, grad_wk, grad_wv, grad_wo, grad_wh])
    grad_token = jnp.stack([grad_hidden_tok, grad_skip_tok])
    grad_vector = jnp.stack(
        [grad_gain_one, grad_gain_two, grad_bias_tok, grad_bias_out, grad_bias_head]
    )
    square_share, ffn_share, token_share, vector_share = (
        lax.psum_scatter(grad_square, ("dp", "head"), scatter_dimension=1, tiled=True),
        lax.psum_scatter(grad_ffn, ("dp", "head"), scatter_dimension=1, tiled=True),
        lax.psum_scatter(grad_token, ("dp", "head"), scatter_dimension=1, tiled=True),
        lax.psum_scatter(grad_vector, ("dp", "head"), scatter_dimension=1, tiled=True),
    )
    head_share = lax.psum_scatter(gradient_of_head, "dp", scatter_dimension=1, tiled=True)
    all_tokens = tok_count * lax.axis_size("dp") * lax.axis_size("head")
    matrix_rate = 0.5 / (D * all_tokens) ** 0.5
    quadratic_params_fresh, quadratic_velocity_fresh, quadratic_mean_fresh = update(
        quadratic_params, quadratic_velocity, quadratic_mean, square_share, matrix_rate
    )
    perceptron_params_fresh, perceptron_velocity_fresh, perceptron_mean_fresh = update(
        perceptron_params, perceptron_velocity, perceptron_mean, ffn_share, matrix_rate
    )
    embedder_params_fresh, embedder_velocity_fresh, embedder_mean_fresh = update(
        embedder_params,
        embedder_velocity,
        embedder_mean,
        token_share,
        0.5 / (2 * PATCH * all_tokens) ** 0.5,
    )
    bias_gain_params_fresh, bias_gain_velocity_fresh, bias_gain_mean_fresh = update(
        bias_gain_params, bias_gain_velocity, bias_gain_mean, vector_share, 0.3 / all_tokens**0.5
    )
    readout_params_fresh, readout_velocity_fresh, readout_mean_fresh = update(
        readout_params, readout_velocity, readout_mean, head_share, matrix_rate
    )
    return (
        prediction,
        segment_derivative,
        quadratic_params_fresh,
        quadratic_velocity_fresh,
        quadratic_mean_fresh,
        perceptron_params_fresh,
        perceptron_velocity_fresh,
        perceptron_mean_fresh,
        embedder_params_fresh,
        embedder_velocity_fresh,
        embedder_mean_fresh,
        bias_gain_params_fresh,
        bias_gain_velocity_fresh,
        bias_gain_mean_fresh,
        readout_params_fresh,
        readout_velocity_fresh,
        readout_mean_fresh,
    )


def solution(mesh):
    placed = (
        P(("dp", "head"), None),
        P(("dp", "head"), None),
        P(("dp", "head")),
        P("dp", "head"),
        P(None, ("dp", "head"), None),
        P(None, ("dp", "head"), None),
        P(None, ("dp", "head"), None),
        P(None, ("dp", "head"), None),
        P(None, ("dp", "head"), None),
        P(None, ("dp", "head"), None),
        P(None, ("dp", "head"), None),
        P(None, ("dp", "head"), None),
        P(None, ("dp", "head"), None),
        P(None, ("dp", "head")),
        P(None, ("dp", "head")),
        P(None, ("dp", "head")),
        P(None, "dp", "head"),
        P(None, "dp", "head"),
        P(None, "dp", "head"),
    )
    return jax.shard_map(
        on_device,
        mesh=mesh,
        in_specs=placed,
        out_specs=(
            P("dp", "head"),
            P(("dp", "head"), None),
            P(None, ("dp", "head"), None),
            P(None, ("dp", "head"), None),
            P(None, ("dp", "head"), None),
            P(None, ("dp", "head"), None),
            P(None, ("dp", "head"), None),
            P(None, ("dp", "head"), None),
            P(None, ("dp", "head"), None),
            P(None, ("dp", "head"), None),
            P(None, ("dp", "head"), None),
            P(None, ("dp", "head")),
            P(None, ("dp", "head")),
            P(None, ("dp", "head")),
            P(None, "dp", "head"),
            P(None, "dp", "head"),
            P(None, "dp", "head"),
        ),
        check_vma=False,
    )
```

profile of v0, /device:TPU:1, one launch (start us, length us, event | category | flops | bytes accessed | tf_op | source)
XLA Modules:
  0.0 1786.6 jit_solution(10228850122551237173)
XLA Ops:
  12.6 46.3 %all-gather.13.cloned.1.call-done = bf16[2,1280,320]{2,1,0:T(8,128)(2,1)} async-done(((bf16[2,160,320]{2,1,0:T(8,128)(2,1)}), bf16[2,1280,320]{2,1,0:T(8,128)(2,1)}) %all-gather.13.cloned.1.call-update) | async-done | bytes 1638416 | tf_op jit(solution)/shard_map/all_gather | solution.py:149
  58.9 5.9 convolution_convert_fusion
  65.5 42.5 %all-gather = bf16[32,40,5]{1,2,0:T(8,128)(2,1)S(1)} all-gather(bf16[1,40,5]{1,2,0:T(8,128)(2,1)S(1)} %convert_bitcast_fusion), channel_id=1, replica_groups=mesh['dp'=8,'head'=4] {'dp','head'}, dimensions={0}, use_global_device_ids=true | all-gather | bytes 13200 | tf_op jit(solution)/shard_map/all_gather | solution.py:147
  108.3 41.0 %all_gather.21 = bf16[2,1280,64]{2,1,0:T(8,128)(2,1)S(1)} all-gather(bf16[2,40,64]{2,1,0:T(8,128)(2,1)S(1)} %convert_element_type.162), channel_id=1, replica_groups=mesh['dp'=8,'head'=4] {'dp','head'}, dimensions={1}, use_global_device_ids=true | all-gather | bytes 337920 | tf_op jit(solution)/shard_map/all_gather | solution.py:146
  152.7 5.9 convolution_convert_fusion.1
  158.6 33.8 %all-gather.7.cloned.1.call-done = bf16[6,1280,1280]{2,1,0:T(8,128)(2,1)} async-done(((bf16[6,40,1280]{2,1,0:T(8,128)(2,1)}), bf16[6,1280,1280]{2,1,0:T(8,128)(2,1)}) %all-gather.7.cloned.1.call-update) | async-done | bytes 19660816 | tf_op jit(solution)/shard_map/all_gather | solution.py:144
  192.3 4.9 fusion.23
  199.4 6.1 slice_bitcast_fusion.25
  205.5 6.0 copy.104
  211.5 5.6 copy.105
  224.7 7.7 fusion.58
  232.4 4.8 convolution_convert_fusion.3
  238.9 8.8 fusion
  247.7 8.2 fusion.29
  256.0 6.0 multiply_reduce_fusion.5
  262.0 93.0 %all-gather.9.cloned.1.call-done = bf16[2,1280,5120]{2,1,0:T(8,128)(2,1)} async-done(((bf16[2,40,5120]{2,1,0:T(8,128)(2,1)}), bf16[2,1280,5120]{2,1,0:T(8,128)(2,1)}) %all-gather.9.cloned.1.call-update) | async-done | bytes 26214416 | tf_op jit(solution)/shard_map/all_gather | solution.py:145
  355.1 13.3 fusion.3
  368.3 17.6 fusion.22
  385.9 20.5 %reduce-scatter.8.cloned.1.call-done = bf16[512,1280]{1,0:T(8,128)(2,1)} async-done(((bf16[2048,1280]{1,0:T(8,128)(2,1)}), bf16[512,1280]{1,0:T(8,128)(2,1)}) %reduce-scatter.8.cloned.1.call-update) | async-done | bytes 1310736 | tf_op jit(solution)/shard_map/reduce_scatter | solution.py:207
  406.4 7.0 convert_reduce_fusion
  414.3 45.9 %reduce-scatter.6.cloned.1.call-done = bf16[512,1280]{1,0:T(8,128)(2,1)} async-done(((bf16[2048,1280]{1,0:T(8,128)(2,1)}), bf16[512,1280]{1,0:T(8,128)(2,1)}) %reduce-scatter.6.cloned.1.call-update) | async-done | bytes 1310736 | tf_op jit(solution)/shard_map/reduce_scatter | solution.py:213
  465.9 15.5 multiply_convert_fusion.1
  481.4 14.8 multiply_reduce_fusion.1
  500.9 4.9 convolution_convert_fusion.2
  507.5 13.1 multiply_reduce_fusion
  520.6 12.6 multiply_convert_fusion
  538.4 4.8 fusion.19
  547.2 8.6 fusion.30
  555.8 4.8 multiply_reduce_fusion.2
  569.8 5.5 convolution_bitcast_fusion.9
  575.3 4.6 convolution_bitcast_fusion.8
  581.9 7.5 copy.114
  589.5 6.6 fusion.11
  596.1 4.6 fusion.10
  600.7 4.7 fusion.9
  610.0 4.7 fusion.7
  614.6 4.6 fusion.6
  619.5 15.1 convolution_bitcast_fusion.1
  634.6 16.4 convolution_bitcast_fusion
  651.0 35.5 %pad_maximum_fusion = f32[2,1280,5120]{2,1,0:T(8,128)} fusion(f32[1,1280,5120]{2,1,0:T(8,128)} %convolution_bitcast_fusion, f32[1,1280,5120]{2,1,0:T(8,128)} %convolution_bitcast_fusion.1), kind=kLoop, calls=%fused_computation | loop fusion | flops 13107200 | bytes 104857600 | tf_op jit(solution)/shard_map/stack | solution.py:230
  688.5 42.4 %all-reduce.1 = f32[5,1280]{1,0:T(8,128)S(1)} all-reduce(f32[5,1280]{1,0:T(8,128)S(1)} %stack.78), channel_id=7, replica_groups=mesh['dp'=8,'head'=4] {'dp','head'}, use_global_device_ids=true, to_apply=%region_17.18.clone | all-reduce | flops 6400 | bytes 51200
  736.9 4.9 fusion.36
  741.8 5.7 fusion.26
  747.5 106.8 %all-reduce.8.cloned.1.call-done = f32[2,1280,320]{2,0,1:T(2,128)} async-done(((f32[2,1280,320]{2,0,1:T(2,128)}), f32[2,1280,320]{2,0,1:T(2,128)}) %all-reduce.8.cloned.1.call-update) | async-done | bytes 3276816
  856.8 361.0 %reduce-scatter.10.cloned.1.call-done = f32[6,40,1280]{2,1,0:T(8,128)} async-done(((f32[6,1280,1280]{2,1,0:T(8,128)}), f32[6,40,1280]{2,1,0:T(8,128)}) %reduce-scatter.10.cloned.1.call-update) | async-done | bytes 1228816 | tf_op jit(solution)/shard_map/reduce_scatter | solution.py:267
  1217.8 4.6 multiply_add_fusion.4
  1222.3 552.1 %reduce-scatter.12.cloned.1.call-done = f32[2,40,5120]{2,1,0:T(8,128)} async-done(((f32[2,1280,5120]{2,1,0:T(8,128)}), f32[2,40,5120]{2,1,0:T(8,128)}) %reduce-scatter.12.cloned.1.call-update) | async-done | bytes 1638416 | tf_op jit(solution)/shard_map/reduce_scatter | solution.py:268
  1774.4 5.2 multiply_add_fusion
  (225 shorter events, 68.1 us)
Async XLA Ops:
  7.2 51.7 %copy-start = (bf16[2048,320]{0,1:T(8,128)(2,1)S(1)}, bf16[2048,320]{0,1:T(8,128)(2,1)}, u32[]{:S(2)}) copy-start(bf16[2048,320]{0,1:T(8,128)(2,1)} %param.22) | copy-start | bytes 3932164
  7.2 51.7 %all-gather.13.cloned.1.call-start = ((), (), s32[]{:S(2)}) async-start(), calls=%async_computation.7 | async-start | bytes 2211840 | tf_op jit(solution)/shard_map/all_gather | solution.py:149
  9.2 183.2 %all-gather.7.cloned.1.call-start = ((), (), s32[]{:S(2)}) async-start(), calls=%async_computation.4 | async-start | bytes 20275200 | tf_op jit(solution)/shard_map/all_gather | solution.py:144
  11.4 343.6 %all-gather.9.cloned.1.call-start = ((), (), s32[]{:S(2)}) async-start(), calls=%async_computation.5 | async-start | bytes 27033600 | tf_op jit(solution)/shard_map/all_gather | solution.py:145
  12.5 393.9 %reduce-scatter.8.cloned.1.call-start = ((), (), s32[]{:S(2)}) async-start(), calls=%async_computation.10 | async-start | bytes 6553600 | tf_op jit(solution)/shard_map/reduce_scatter | solution.py:207
  64.7 84.5 %copy-start.46 = (s32[512,32]{0,1:T(8,128)S(1)}, s32[512,32]{0,1:T(8,128)}, u32[]{:S(2)}) copy-start(s32[512,32]{0,1:T(8,128)} %param.20) | copy-start | bytes 196612
  64.8 84.6 %copy-start.55 = (f32[512,32]{0,1:T(8,128)S(1)}, f32[512,32]{0,1:T(8,128)}, u32[]{:S(2)}) copy-start(f32[512,32]{0,1:T(8,128)} %param.19) | copy-start | bytes 196612
  64.8 85.6 %copy-start.64 = (s32[512]{0:T(512)S(1)}, s32[512]{0:T(512)}, u32[]{:S(2)}) copy-start(s32[512]{0:T(512)} %param.21) | copy-start | bytes 6148
  64.8 395.4 %reduce-scatter.6.cloned.1.call-start = ((), (), s32[]{:S(2)}) async-start(), calls=%async_computation.9 | async-start | bytes 6553600 | tf_op jit(solution)/shard_map/reduce_scatter | solution.py:213
  108.3 108.9 %copy-start.53 = (f32[1280]{0:T(1024)}, f32[1280]{0:T(1024)S(1)}, u32[]{:S(2)}) copy-start(f32[1280]{0:T(1024)S(1)} %get-tuple-element.125) | copy-start | bytes 15364
  149.3 48.0 %copy-start.11 = (bf16[2,1280,64]{2,1,0:T(8,128)(2,1)}, bf16[2,1280,64]{2,1,0:T(8,128)(2,1)S(1)}, u32[]{:S(2)}) copy-start(bf16[2,1280,64]{2,1,0:T(8,128)(2,1)S(1)} %all_gather.21) | copy-start | bytes 983044
  149.3 48.0 %copy-start.40 = (bf16[512,32]{0,1:T(8,128)(2,1)}, bf16[512,32]{0,1:T(8,128)(2,1)S(1)}, u32[]{:S(2)}) copy-start(bf16[512,32]{0,1:T(8,128)(2,1)S(1)} %convert_convert_fusion) | copy-start | bytes 98308
  149.4 47.9 %copy-start.42 = (bf16[512,32]{0,1:T(8,128)(2,1)}, bf16[512,32]{0,1:T(8,128)(2,1)S(1)}, u32[]{:S(2)}) copy-start(bf16[512,32]{0,1:T(8,128)(2,1)S(1)} %multiply_convert_fusion.8) | copy-start | bytes 98308
  150.4 73.5 %copy-start.44 = (f32[512,40]{0,1:T(8,128)}, f32[512,40]{0,1:T(8,128)S(1)}, u32[]{:S(2)}) copy-start(f32[512,40]{0,1:T(8,128)S(1)} %get-tuple-element.164) | copy-start | bytes 245764
  158.5 411.2 %all-gather.11.cloned.1.call-start = ((), (), s32[]{:S(2)}) async-start(), calls=%async_computation.6 | async-start | bytes 6553600 | tf_op jit(solution)/shard_map/all_gather | solution.py:194
  199.4 17.8 copy-start.60
  219.3 13.1 copy-start.32
  224.7 7.7 copy-start.17
  224.7 7.7 copy-start.19
  224.7 7.7 copy-start.21
  224.7 7.7 copy-start.23
  238.9 8.8 copy-start.13
  247.7 8.3 copy-start.1
  385.9 27.5 %copy-start.38 = (bf16[512,1280]{1,0:T(8,128)(2,1)}, bf16[512,1280]{1,0:T(8,128)(2,1)S(1)}, u32[]{:S(2)}) copy-start(bf16[512,1280]{1,0:T(8,128)(2,1)S(1)} %fusion.22) | copy-start | bytes 3932164
  413.4 46.7 %copy-start.70 = (bf16[512,1280]{1,0:T(8,128)(2,1)S(1)}, bf16[512,1280]{1,0:T(8,128)(2,1)}, u32[]{:S(2)}) copy-start(bf16[512,1280]{1,0:T(8,128)(2,1)} %get-tuple-element.135) | copy-start | bytes 3932164
  413.5 161.8 %all-gather.15.cloned.1.call-start = ((), (), s32[]{:S(2)}) async-start(), calls=%async_computation.8 | async-start | bytes 6553600 | tf_op jit(solution)/shard_map/all_gather | solution.py:193
  414.2 321.2 %all-reduce.6.cloned.1.call-start = ((), (), s32[]{:S(2)}) async-start(), calls=%async_computation.13 | async-start | bytes 2621440
  465.9 15.5 copy-start.6
  520.6 12.6 copy-start.22
  520.6 12.6 copy-start.24
  547.2 8.6 copy-start.2
  547.2 8.6 copy-start.54
  547.2 8.6 copy-start.61
  569.7 284.6 %all-reduce.8.cloned.1.call-start = ((), (), s32[]{:S(2)}) async-start(), calls=%async_computation.14 | async-start | bytes 7864320
  589.4 628.3 %reduce-scatter.10.cloned.1.call-start = ((), (), s32[]{:S(2)}) async-start(), calls=%async_computation.11 | async-start | bytes 40550400 | tf_op jit(solution)/shard_map/reduce_scatter | solution.py:267
  619.3 1155.2 %reduce-scatter.12.cloned.1.call-start = ((), (), s32[]{:S(2)}) async-start(), calls=%async_computation.12 | async-start | bytes 54067200 | tf_op jit(solution)/shard_map/reduce_scatter | solution.py:268
  619.5 15.1 copy-start.27
  686.5 44.4 %copy-start.63 = (f32[5,40]{1,0:T(8,128)S(1)}, f32[5,40]{1,0:T(8,128)}, u32[]{:S(2)}) copy-start(f32[5,40]{1,0:T(8,128)} %param.32) | copy-start | bytes 2404
  686.5 44.4 %copy-start.67 = (f32[5,40]{1,0:T(8,128)S(1)}, f32[5,40]{1,0:T(8,128)}, u32[]{:S(2)}) copy-start(f32[5,40]{1,0:T(8,128)} %param.34) | copy-start | bytes 2404
  686.6 45.8 %copy-start.12 = (bf16[2,1280,64]{2,1,0:T(8,128)(2,1)S(1)}, bf16[2,1280,64]{2,1,0:T(8,128)(2,1)}, u32[]{:S(2)}) copy-start(bf16[2,1280,64]{2,1,0:T(8,128)(2,1)} %copy-done.11) | copy-start | bytes 983044
  686.6 48.2 %copy-start.47 = (s32[512,32]{0,1:T(8,128)S(1)}, s32[512,32]{0,1:T(8,128)}, u32[]{:S(2)}) copy-start(s32[512,32]{0,1:T(8,128)} %param.20) | copy-start | bytes 196612
  686.6 49.6 %copy-start.52 = (f32[2,40,64]{2,1,0:T(8,128)S(1)}, f32[2,40,64]{2,1,0:T(8,128)}, u32[]{:S(2)}) copy-start(f32[2,40,64]{2,1,0:T(8,128)} %param.29) | copy-start | bytes 61444
  686.6 49.6 %copy-start.56 = (f32[2,40,64]{2,1,0:T(8,128)S(1)}, f32[2,40,64]{2,1,0:T(8,128)}, u32[]{:S(2)}) copy-start(f32[2,40,64]{2,1,0:T(8,128)} %param.31) | copy-start | bytes 61444
  686.6 49.6 %copy-start.57 = (f32[2,40,64]{2,1,0:T(8,128)S(1)}, f32[2,40,64]{2,1,0:T(8,128)}, u32[]{:S(2)}) copy-start(f32[2,40,64]{2,1,0:T(8,128)} %param.30) | copy-start | bytes 61444
  741.8 113.8 %copy-start.28 = (f32[2,160,320]{2,1,0:T(8,128)S(1)}, f32[2,160,320]{2,1,0:T(8,128)}, u32[]{:S(2)}) copy-start(f32[2,160,320]{2,1,0:T(8,128)} %param.35) | copy-start | bytes 1228804
  741.8 113.8 %copy-start.48 = (f32[2,160,320]{2,1,0:T(8,128)S(1)}, f32[2,160,320]{2,1,0:T(8,128)}, u32[]{:S(2)}) copy-start(f32[2,160,320]{2,1,0:T(8,128)} %param.37) | copy-start | bytes 1228804
  741.8 113.8 %copy-start.49 = (f32[2,160,320]{2,1,0:T(8,128)S(1)}, f32[2,160,320]{2,1,0:T(8,128)}, u32[]{:S(2)}) copy-start(f32[2,160,320]{2,1,0:T(8,128)} %param.36) | copy-start | bytes 1228804
  856.8 917.6 %copy-start.8 = (f32[2,40,5120]{2,1,0:T(8,128)S(1)}, f32[2,40,5120]{2,1,0:T(8,128)}, u32[]{:S(2)}) copy-start(f32[2,40,5120]{2,1,0:T(8,128)} %param.26) | copy-start | bytes 4915204
  (35 other events, 117.5 us)
Sparse Core Ops, SparseCore 0:
  10.8 48.0 all-gather.12
  62.3 129.9 all-gather.6
  195.8 159.1 all-gather.8
  357.4 48.9 reduce-scatter.7
  408.8 51.3 reduce-scatter.5
  462.1 40.9 all-gather.10
  505.3 40.3 all-gather.14
  569.8 131.4 all-reduce.5
  704.9 149.3 all-reduce.7
  860.6 357.1 reduce-scatter.9
  1220.1 554.3 reduce-scatter.11
where the time goes:
time: 1790 us
  waiting for transfers between devices  1260 us (70%)
  matrix products  257 us (14%)
  blocking collectives  126 us (7%)
  other arithmetic  87.1 us (5%)
  local copies, waits for them, and re-layouts  39.3 us (2%)
    reduce_scatter x1, waiting for transfers between devices, on_device(): lax.psum_scatter(grad_ffn, ('dp', 'head'), scatter_dimension=1, tiled=True)  552 us
    reduce_scatter x1, waiting for transfers between devices, on_device(): lax.psum_scatter(grad_square, ('dp', 'head'), scatter_dimension=1, tiled=...  361 us
    unnamed x13, waiting for transfers between devices  108 us
    all_gather x1, waiting for transfers between devices, on_device(): lax.all_gather(rounded(perceptron_params), ('dp', 'head'), axis=1, tiled=...  93 us
    dot_general x12, matrix products, flipped_bilinear(): lax.dot_general(left_mat, right_mat, (((1,), (1,)), ((), ())), preferred_...  75.2 us
    dot_general x12, matrix products, bilinear_flipped(): lax.dot_general(left_mat, right_mat, (((0,), (0,)), ((), ())), preferred_...  72 us
    dot_general x12, matrix products, matrix_multiply(): return jnp.dot(left_mat, right_mat, preferred_element_type=jnp.float32)  68.5 us
    all_gather x1, waiting for transfers between devices, on_device(): lax.all_gather(rounded(readout_params), 'dp', axis=1, tiled=True)  46.3 us
  transfers between devices with their start and end apart: 11, of which 8 were waited for; matrix products, arithmetic and copies ran while one was open for 21% of the time, Pallas kernels for 0%

commit v1 on v0

--- a/solution.py
+++ b/solution.py
@@ -146,7 +146,25 @@
         lax.all_gather(rounded(embedder_params), ("dp", "head"), axis=1, tiled=True),
         lax.all_gather(rounded(bias_gain_params), ("dp", "head"), axis=1, tiled=True),
     )
-    readout_outcome = lax.all_gather(rounded(readout_params), "dp", axis=1, tiled=True)
+    value = rounded(readout_params)
+    size, index, width = (lax.axis_size("dp"), lax.axis_index("dp"), value.shape[1])
+    forward = [(i, (i + 1) % size) for i in range(size)]
+    backward = [(i, (i - 1) % size) for i in range(size)]
+    filled = jnp.zeros((*value.shape[:1], size * width, *value.shape[1 + 1 :]), value.dtype)
+    filled = lax.dynamic_update_slice_in_dim(filled, value, index * width, axis=1)
+    from_left = from_right = value
+    halfway = size // 2
+    for step in range(1, halfway + 1):
+        from_left = lax.ppermute(from_left, "dp", forward)
+        filled = lax.dynamic_update_slice_in_dim(
+            filled, from_left, (index - step) % size * width, axis=1
+        )
+        if step < size - halfway:
+            from_right = lax.ppermute(from_right, "dp", backward)
+            filled = lax.dynamic_update_slice_in_dim(
+                filled, from_right, (index + step) % size * width, axis=1
+            )
+    readout_outcome = filled
     vectors = vector_low.astype(jnp.float32)
     tok_count = input_segments.shape[0]
     seq_rows = tok_count // SEQ

time: 1790 us -> 1710 us (0.955)
  waiting for transfers between devices: 1260 us -> 1140 us
    all_gather x1 -> x0, waiting for transfers between devices: 46.3 us -> none  [on_device(): lax.all_gather(rounded(readout_params), 'dp', axis=1, tiled=True)]
    reduce_scatter x1, waiting for transfers between devices: 45.9 us -> 0.01 us  [on_device(): lax.psum_scatter(flipped_bilinear(prediction_adjoint, readout_outcome[1])...]
    ppermute x0 -> x7, waiting for transfers between devices: none -> 34.1 us  [the longest x4 34.1 us: on_device(): from_left = lax.ppermute(from_left, 'dp', forward)]
    all_gather x1, waiting for transfers between devices: 33.8 us -> 0.02 us  [on_device(): lax.all_gather(rounded(quadratic_params), ('dp', 'head'), axis=1, tiled=T...]
    reduce_scatter x1, waiting for transfers between devices: 20.5 us -> 0.01 us  [on_device(): lax.psum_scatter(flipped_bilinear(prediction_adjoint, readout_outcome[0])...]
    unnamed x13 -> x12, waiting for transfers between devices: 108 us -> 106 us
  transfers between devices with their start and end apart: 11 -> 17, of which waited for: 8 -> 8; matrix products, arithmetic and copies ran while one was open for 21% -> 22% of each run, Pallas kernels for 0% -> 0%
where the time goes in v1:
time: 1710 us; the launch traced here: 1700 us
  waiting for transfers between devices  1140 us (67%)
  matrix products  260 us (15%)
  blocking collectives  126 us (7%)
  other arithmetic  89 us (5%)
  local copies, waits for them, and re-layouts  49.3 us (3%)
  starting transfers between devices  18.4 us (1%)
  between operations  18 us (1%)
    reduce_scatter x1, waiting for transfers between devices, on_device(): lax.psum_scatter(grad_ffn, ('dp', 'head'), scatter_dimension=1, tiled=True)  552 us
    reduce_scatter x1, waiting for transfers between devices, on_device(): lax.psum_scatter(grad_square, ('dp', 'head'), scatter_dimension=1, tiled=...  361 us
    unnamed x12, waiting for transfers between devices  106 us
    all_gather x1, waiting for transfers between devices, on_device(): lax.all_gather(rounded(perceptron_params), ('dp', 'head'), axis=1, tiled=...  86.7 us
    dot_general x12, matrix products, flipped_bilinear(): lax.dot_general(left_mat, right_mat, (((1,), (1,)), ((), ())), preferred_...  74 us
    dot_general x12, matrix products, matrix_multiply(): return jnp.dot(left_mat, right_mat, preferred_element_type=jnp.float32)  73.3 us
    dot_general x12, matrix products, bilinear_flipped(): lax.dot_general(left_mat, right_mat, (((0,), (0,)), ((), ())), preferred_...  72 us
    all_gather x1, blocking collectives, on_device(): lax.all_gather(rounded(bias_gain_params), ('dp', 'head'), axis=1, tiled=T...  44.6 us
  transfers between devices with their start and end apart: 17, of which 8 were waited for; matrix products, arithmetic and copies ran while one was open for 22% of the time, Pallas kernels for 0%

profile of v1, /device:TPU:1, one launch (start us, length us, event | category | flops | bytes accessed | tf_op | source)
XLA Modules:
  0.0 1701.1 jit_solution(16208926462721517744)
XLA Ops:
  18.2 8.0 collective-permute-done
  33.8 8.3 collective-permute-done.2
  47.8 6.7 collective-permute-done.4
  58.2 11.1 collective-permute-done.6
  70.0 5.9 fusion.17
  76.7 44.6 %all-gather = bf16[32,40,5]{1,2,0:T(8,128)(2,1)S(1)} all-gather(bf16[1,40,5]{1,2,0:T(8,128)(2,1)S(1)} %convert_bitcast_fusion), channel_id=1, replica_groups=mesh['dp'=8,'head'=4] {'dp','head'}, dimensions={0}, use_global_device_ids=true | all-gather | bytes 13200 | tf_op jit(solution)/shard_map/all_gather | solution.py:147
  121.5 41.7 %all_gather.18 = bf16[2,1280,64]{2,1,0:T(8,128)(2,1)S(1)} all-gather(bf16[2,40,64]{2,1,0:T(8,128)(2,1)S(1)} %convert_element_type.168), channel_id=1, replica_groups=mesh['dp'=8,'head'=4] {'dp','head'}, dimensions={1}, use_global_device_ids=true | all-gather | bytes 337920 | tf_op jit(solution)/shard_map/all_gather | solution.py:146
  166.5 5.9 fusion.16
  172.5 5.3 fusion.25
  181.3 5.4 convolution_convert_fusion.3
  188.5 6.7 slice_bitcast_fusion.25
  195.2 5.8 copy.110
  201.0 5.8 convolution_bitcast_fusion.13
  206.8 5.6 copy.111
  217.7 7.5 fusion.60
  225.2 8.3 fusion
  233.6 8.3 fusion.31
  241.9 5.9 multiply_reduce_fusion.5
  247.8 86.7 %all-gather.8.cloned.1.call-done = bf16[2,1280,5120]{2,1,0:T(8,128)(2,1)} async-done(((bf16[2,40,5120]{2,1,0:T(8,128)(2,1)}), bf16[2,1280,5120]{2,1,0:T(8,128)(2,1)}) %all-gather.8.cloned.1.call-update) | async-done | bytes 26214416 | tf_op jit(solution)/shard_map/all_gather | solution.py:145
  334.5 13.1 fusion.3
  347.7 17.8 %fusion.24 = bf16[512,1280]{1,0:T(8,128)(2,1)} fusion(f32[512,1280]{1,0:T(8,128)} %get-tuple-element.172, bf16[2,1280,5120]{2,1,0:T(8,128)(2,1)} %all-gather.8.cloned.1.call-done, f32[512,5120]{1,0:T(8,128)} %fusion.3), kind=kOutput, calls=%fused_computation.62 | convolution fusion | flops 6725304320 | bytes 27525120 | tf_op jit(solution)/shard_map/dot_general | solution.py:21
  365.6 5.7 convolution_add_fusion.5
  371.3 5.6 convert_reduce_fusion
  383.6 14.7 multiply_convert_fusion.1
  398.3 14.9 multiply_reduce_fusion.1
  417.9 4.9 convolution_convert_fusion.2
  424.5 12.8 multiply_reduce_fusion
  437.3 12.6 multiply_convert_fusion
  455.1 4.8 fusion.21
  463.8 8.6 fusion.32
  472.5 4.8 multiply_reduce_fusion.2
  486.4 5.5 convolution_bitcast_fusion.8
  498.4 7.5 copy.122
  506.0 6.6 fusion.11
  512.6 4.6 fusion.10
  517.3 4.7 fusion.9
  526.5 4.7 fusion.7
  531.2 4.6 fusion.6
  536.1 15.0 convolution_bitcast_fusion.1
  551.1 16.4 convolution_bitcast_fusion
  567.6 35.9 %pad_maximum_fusion = f32[2,1280,5120]{2,1,0:T(8,128)} fusion(f32[1,1280,5120]{2,1,0:T(8,128)} %convolution_bitcast_fusion, f32[1,1280,5120]{2,1,0:T(8,128)} %convolution_bitcast_fusion.1), kind=kLoop, calls=%fused_computation | loop fusion | flops 13107200 | bytes 104857600 | tf_op jit(solution)/shard_map/stack | solution.py:248
  605.5 40.0 %all-reduce.1 = f32[5,1280]{1,0:T(8,128)S(1)} all-reduce(f32[5,1280]{1,0:T(8,128)S(1)} %stack.78), channel_id=7, replica_groups=mesh['dp'=8,'head'=4] {'dp','head'}, use_global_device_ids=true, to_apply=%region_17.18.clone | all-reduce | flops 6400 | bytes 51200
  651.4 4.9 fusion.38
  656.4 5.7 fusion.28
  662.0 105.9 %all-reduce.8.cloned.1.call-done = f32[2,1280,320]{2,0,1:T(2,128)} async-done(((f32[2,1280,320]{2,0,1:T(2,128)}), f32[2,1280,320]{2,0,1:T(2,128)}) %all-reduce.8.cloned.1.call-update) | async-done | bytes 3276816
  770.4 361.0 %reduce-scatter.10.cloned.1.call-done = f32[6,40,1280]{2,1,0:T(8,128)} async-done(((f32[6,1280,1280]{2,1,0:T(8,128)}), f32[6,40,1280]{2,1,0:T(8,128)}) %reduce-scatter.10.cloned.1.call-update) | async-done | bytes 1228816 | tf_op jit(solution)/shard_map/reduce_scatter | solution.py:285
  1136.0 552.0 %reduce-scatter.12.cloned.1.call-done = f32[2,40,5120]{2,1,0:T(8,128)} async-done(((f32[2,1280,5120]{2,1,0:T(8,128)}), f32[2,40,5120]{2,1,0:T(8,128)}) %reduce-scatter.12.cloned.1.call-update) | async-done | bytes 1638416 | tf_op jit(solution)/shard_map/reduce_scatter | solution.py:286
  1687.9 5.2 multiply_add_fusion
  (247 shorter events, 99.2 us)
Async XLA Ops:
  8.0 62.0 %copy-start = (bf16[2048,320]{0,1:T(8,128)(2,1)S(1)}, bf16[2048,320]{0,1:T(8,128)(2,1)}, u32[]{:S(2)}) copy-start(bf16[2048,320]{0,1:T(8,128)(2,1)} %param.22) | copy-start | bytes 3932164
  8.0 164.4 %all-gather.6.cloned.1.call-start = ((), (), s32[]{:S(2)}) async-start(), calls=%async_computation.4 | async-start | bytes 20275200 | tf_op jit(solution)/shard_map/all_gather | solution.py:144
  10.5 324.1 %all-gather.8.cloned.1.call-start = ((), (), s32[]{:S(2)}) async-start(), calls=%async_computation.5 | async-start | bytes 27033600 | tf_op jit(solution)/shard_map/all_gather | solution.py:145
  11.5 359.7 %reduce-scatter.8.cloned.1.call-start = ((), (), s32[]{:S(2)}) async-start(), calls=%async_computation.9 | async-start | bytes 6553600 | tf_op jit(solution)/shard_map/reduce_scatter | solution.py:225
  13.1 13.1 collective-permute-start
  15.1 13.4 collective-permute-start.1
  26.2 16.0 collective-permute-start.2
  28.5 13.7 collective-permute-start.3
  42.1 12.3 collective-permute-start.4
  42.1 15.4 collective-permute-start.5
  54.5 14.8 collective-permute-start.6
  75.9 87.3 %copy-start.50 = (s32[512,32]{0,1:T(8,128)S(1)}, s32[512,32]{0,1:T(8,128)}, u32[]{:S(2)}) copy-start(s32[512,32]{0,1:T(8,128)} %param.20) | copy-start | bytes 196612
  75.9 87.3 %copy-start.59 = (f32[512,32]{0,1:T(8,128)S(1)}, f32[512,32]{0,1:T(8,128)}, u32[]{:S(2)}) copy-start(f32[512,32]{0,1:T(8,128)} %param.19) | copy-start | bytes 196612
  75.9 88.4 %copy-start.69 = (s32[512]{0:T(512)S(1)}, s32[512]{0:T(512)}, u32[]{:S(2)}) copy-start(s32[512]{0:T(512)} %param.21) | copy-start | bytes 6148
  75.9 300.9 %reduce-scatter.6.cloned.1.call-start = ((), (), s32[]{:S(2)}) async-start(), calls=%async_computation.8 | async-start | bytes 6553600 | tf_op jit(solution)/shard_map/reduce_scatter | solution.py:231
  121.5 57.1 %copy-start.57 = (f32[1280]{0:T(1024)}, f32[1280]{0:T(1024)S(1)}, u32[]{:S(2)}) copy-start(f32[1280]{0:T(1024)S(1)} %get-tuple-element.125) | copy-start | bytes 15364
  163.2 14.6 copy-start.12
  163.2 14.6 copy-start.44
  163.2 14.5 copy-start.46
  164.3 52.5 %copy-start.48 = (f32[512,40]{0,1:T(8,128)}, f32[512,40]{0,1:T(8,128)S(1)}, u32[]{:S(2)}) copy-start(f32[512,40]{0,1:T(8,128)S(1)} %get-tuple-element.166) | copy-start | bytes 245764
  172.4 314.0 %all-gather.12.cloned.1.call-start = ((), (), s32[]{:S(2)}) async-start(), calls=%async_computation.7 | async-start | bytes 6553600 | tf_op jit(solution)/shard_map/all_gather | solution.py:211
  188.5 45.1 %copy-start.14 = (bf16[512,1280]{0,1:T(8,128)(2,1)}, bf16[512,1280]{0,1:T(8,128)(2,1)S(1)}, u32[]{:S(2)}) copy-start(bf16[512,1280]{0,1:T(8,128)(2,1)S(1)} %copy.109) | copy-start | bytes 3932164
  217.6 7.6 copy-start.16
  217.6 7.6 copy-start.18
  233.5 8.3 copy-start.2
  365.5 126.4 %all-gather.10.cloned.1.call-start = ((), (), s32[]{:S(2)}) async-start(), calls=%async_computation.6 | async-start | bytes 6553600 | tf_op jit(solution)/shard_map/all_gather | solution.py:212
  383.6 14.7 copy-start.7
  424.4 225.5 %all-reduce.6.cloned.1.call-start = ((), (), s32[]{:S(2)}) async-start(), calls=%async_computation.12 | async-start | bytes 2621440
  437.2 12.6 copy-start.21
  437.3 12.6 copy-start.23
  463.8 8.6 copy-start.3
  463.8 8.6 copy-start.58
  463.8 8.6 copy-start.66
  486.3 281.6 %all-reduce.8.cloned.1.call-start = ((), (), s32[]{:S(2)}) async-start(), calls=%async_computation.13 | async-start | bytes 7864320
  505.9 625.5 %reduce-scatter.10.cloned.1.call-start = ((), (), s32[]{:S(2)}) async-start(), calls=%async_computation.10 | async-start | bytes 40550400 | tf_op jit(solution)/shard_map/reduce_scatter | solution.py:285
  535.8 1152.1 %reduce-scatter.12.cloned.1.call-start = ((), (), s32[]{:S(2)}) async-start(), calls=%async_computation.11 | async-start | bytes 54067200 | tf_op jit(solution)/shard_map/reduce_scatter | solution.py:286
  536.1 15.1 copy-start.27
  603.5 42.0 %copy-start.68 = (f32[5,40]{1,0:T(8,128)S(1)}, f32[5,40]{1,0:T(8,128)}, u32[]{:S(2)}) copy-start(f32[5,40]{1,0:T(8,128)} %param.32) | copy-start | bytes 2404
  603.5 42.0 %copy-start.71 = (f32[5,40]{1,0:T(8,128)S(1)}, f32[5,40]{1,0:T(8,128)}, u32[]{:S(2)}) copy-start(f32[5,40]{1,0:T(8,128)} %param.34) | copy-start | bytes 2404
  603.5 43.4 %copy-start.13 = (bf16[2,1280,64]{2,1,0:T(8,128)(2,1)S(1)}, bf16[2,1280,64]{2,1,0:T(8,128)(2,1)}, u32[]{:S(2)}) copy-start(bf16[2,1280,64]{2,1,0:T(8,128)(2,1)} %copy-done.12) | copy-start | bytes 983044
  603.5 45.7 %copy-start.51 = (s32[512,32]{0,1:T(8,128)S(1)}, s32[512,32]{0,1:T(8,128)}, u32[]{:S(2)}) copy-start(s32[512,32]{0,1:T(8,128)} %param.20) | copy-start | bytes 196612
  603.5 47.2 %copy-start.56 = (f32[2,40,64]{2,1,0:T(8,128)S(1)}, f32[2,40,64]{2,1,0:T(8,128)}, u32[]{:S(2)}) copy-start(f32[2,40,64]{2,1,0:T(8,128)} %param.29) | copy-start | bytes 61444
  603.6 47.1 %copy-start.60 = (f32[2,40,64]{2,1,0:T(8,128)S(1)}, f32[2,40,64]{2,1,0:T(8,128)}, u32[]{:S(2)}) copy-start(f32[2,40,64]{2,1,0:T(8,128)} %param.31) | copy-start | bytes 61444
  603.6 47.1 %copy-start.61 = (f32[2,40,64]{2,1,0:T(8,128)S(1)}, f32[2,40,64]{2,1,0:T(8,128)}, u32[]{:S(2)}) copy-start(f32[2,40,64]{2,1,0:T(8,128)} %param.30) | copy-start | bytes 61444
  656.3 112.8 %copy-start.29 = (f32[2,160,320]{2,1,0:T(8,128)S(1)}, f32[2,160,320]{2,1,0:T(8,128)}, u32[]{:S(2)}) copy-start(f32[2,160,320]{2,1,0:T(8,128)} %param.35) | copy-start | bytes 1228804
  656.4 112.8 %copy-start.52 = (f32[2,160,320]{2,1,0:T(8,128)S(1)}, f32[2,160,320]{2,1,0:T(8,128)}, u32[]{:S(2)}) copy-start(f32[2,160,320]{2,1,0:T(8,128)} %param.37) | copy-start | bytes 1228804
  656.4 112.8 %copy-start.53 = (f32[2,160,320]{2,1,0:T(8,128)S(1)}, f32[2,160,320]{2,1,0:T(8,128)}, u32[]{:S(2)}) copy-start(f32[2,160,320]{2,1,0:T(8,128)} %param.36) | copy-start | bytes 1228804
  770.4 917.5 %copy-start.9 = (f32[2,40,5120]{2,1,0:T(8,128)S(1)}, f32[2,40,5120]{2,1,0:T(8,128)}, u32[]{:S(2)}) copy-start(f32[2,40,5120]{2,1,0:T(8,128)} %param.26) | copy-start | bytes 4915204
  (42 other events, 134.1 us)
Sparse Core Ops, SparseCore 0:
  12.3 149.7 all-gather.5
  165.6 168.8 all-gather.7
  486.4 128.5 all-reduce.5
  618.5 149.4 all-reduce.7
  774.2 357.1 reduce-scatter.9
  1133.6 554.3 reduce-scatter.11
Sparse Core Ops, SparseCore 1:
  76.0 93.1 reduce-scatter.7
  172.5 50.1 reduce-scatter.5
  365.6 38.4 all-gather.11
  424.5 38.4 all-gather.9
